TPU v7x, 32 devices: a whole 2x2x4 slice. The times are simulated.
32 devices in a mesh: dp: 8 (over z, x), tensor: 4 (over y, core).
Axes of the slice: x: 2, y: 2, z: 4, core: 2. Of those that a mesh axis runs over, the one named last changes fastest.
Arguments:
- layer_input: bfloat16 [5120, 2304], P(('dp', 'tensor')), may hold values from -6 to 6
- cotangent: bfloat16 [5120, 2304], P(('dp', 'tensor')), may hold values from -6 to 6
- norm_gains: bfloat16 [4, 2304], replicated, may hold values from 0.25 to 1.75
- w_query: bfloat16 [2304, 2048], P('dp', 'tensor'), may hold values from -0.125 to 0.125
- w_key: bfloat16 [2304, 1024], P('dp', 'tensor'), may hold values from -0.125 to 0.125
- w_value: bfloat16 [2304, 1024], P('dp', 'tensor'), may hold values from -0.125 to 0.125
- w_output: bfloat16 [2048, 2304], P('tensor', 'dp'), may hold values from -0.125 to 0.125
- w_gate: bfloat16 [2304, 9216], P('dp', 'tensor'), may hold values from -0.125 to 0.125
- w_up: bfloat16 [2304, 9216], P('dp', 'tensor'), may hold values from -0.125 to 0.125
- w_down: bfloat16 [9216, 2304], P('tensor', 'dp'), may hold values from -0.0625 to 0.0625
- query_shrink: bfloat16 [8, 16, 2304], replicated, may hold values from -0.125 to 0.125
- key_shrink: bfloat16 [8, 16, 2304], replicated, may hold values from -0.125 to 0.125
- value_shrink: bfloat16 [8, 16, 2304], replicated, may hold values from -0.125 to 0.125
- output_shrink: bfloat16 [8, 16, 2048], P(None, None, 'tensor'), may hold values from -0.125 to 0.125
- gate_shrink: bfloat16 [8, 16, 2304], replicated, may hold values from -0.125 to 0.125
- up_shrink: bfloat16 [8, 16, 2304], replicated, may hold values from -0.125 to 0.125
- down_shrink: bfloat16 [8, 16, 9216], P(None, None, 'tensor'), may hold values from -0.0625 to 0.0625
- query_expand: bfloat16 [8, 16, 2048], P(None, None, 'tensor'), may hold values from -0.75 to 0.75
- key_expand: bfloat16 [8, 16, 1024], P(None, None, 'tensor'), may hold values from -0.75 to 0.75
- value_expand: bfloat16 [8, 16, 1024], P(None, None, 'tensor'), may hold values from -0.75 to 0.75
- output_expand: bfloat16 [8, 16, 2304], replicated, may hold values from -0.75 to 0.75
- gate_expand: bfloat16 [8, 16, 9216], P(None, None, 'tensor'), may hold values from -0.75 to 0.75
- up_expand: bfloat16 [8, 16, 9216], P(None, None, 'tensor'), may hold values from -0.75 to 0.75
- down_expand: bfloat16 [8, 16, 2304], replicated, may hold values from -0.75 to 0.75
- adapter_ids: int32 [8], P('dp'), may hold values from 0 to 7
- parent_segments: int32 [8, 13], P('dp'), may hold values from 0 to 4, as said below
- segment_ids: int32 [5120], P('dp'), may hold values from 0 to 12, as said below
Outputs:
- layer_output: bfloat16 [5120, 2304], P(('dp', 'tensor'))
- input_grad: float32 [5120, 2304], P(('dp', 'tensor'))
- shrink_query: float32 [8, 16, 2304], replicated
- shrink_key: float32 [8, 16, 2304], replicated
- shrink_value: float32 [8, 16, 2304], replicated
- shrink_output: float32 [8, 16, 2048], P(None, None, 'tensor')
- shrink_gate: float32 [8, 16, 2304], replicated
- shrink_up: float32 [8, 16, 2304], replicated
- shrink_down: float32 [8, 16, 9216], P(None, None, 'tensor')
- expand_query: float32 [8, 16, 2048], P(None, None, 'tensor')
- expand_key: float32 [8, 16, 1024], P(None, None, 'tensor')
- expand_value: float32 [8, 16, 1024], P(None, None, 'tensor')
- expand_output: float32 [8, 16, 2304], replicated
- expand_gate: float32 [8, 16, 9216], P(None, None, 'tensor')
- expand_up: float32 [8, 16, 9216], P(None, None, 'tensor')
- expand_down: float32 [8, 16, 2304], replicated
Inputs may be any that keep to these rules, and one draw needn't show every extreme that they name: `parent_segments`: in each tree, segment 0 is the trunk and is its own parent; segments 1 to 4 have parent 0; each of the other segments has a branch (1 to 4) as parent, and every branch is the parent of exactly 2 of them. `segment_ids`: the first 256 tokens of each tree are segment 0; the rest are 12 contiguous runs of 32 tokens, one run for each other segment, in any order.
All inputs are finite; a program needn't handle non-finite values.
Results may differ from a plain program's by a relative error of at most 0.028.
Values may be sent and summed in bfloat16 or wider, within the bound.
No kernel may reach another device: no remote copies, remote signals or barrier semaphores. Data moves between devices by JAX's collectives and lax.ppermute only.
A program may use at most 256 MiB of HBM per device.

v0:
```python
import math
import jax
import jax.numpy as jnp
from jax import lax
from jax.sharding import PartitionSpec as P

HEAD_WIDTH = 256
ADAPTERS = 8


def rms_scale(value_rows, gain_row):
    inverse = lax.rsqrt(jnp.mean(value_rows * value_rows, axis=-1, keepdims=True) + 1e-06)
    return value_rows * inverse * gain_row


def rms_back(value_rows, gain_row, upstream):
    inverse = lax.rsqrt(jnp.mean(value_rows * value_rows, axis=-1, keepdims=True) + 1e-06)
    scaled = gain_row * upstream
    return inverse * scaled - value_rows * (inverse * inverse * inverse) * jnp.mean(
        value_rows * scaled, axis=-1, keepdims=True
    )


def pick_from(lookup, indices, labels):
    return jnp.sum(jnp.where(indices[:, None] == labels[None, :], lookup[None, :], 0), axis=1)


def tree_tables(segments, parents):
    count_seg = parents.shape[0]
    sequence_length = segments.shape[0]
    labels = jnp.arange(count_seg, dtype=jnp.int32)
    places = jnp.arange(sequence_length, dtype=jnp.int32)
    member = segments[None, :] == labels[:, None]
    starts = jnp.min(jnp.where(member, places[None, :], sequence_length), axis=1)
    counts = jnp.sum(member.astype(jnp.int32), axis=1)
    grands = pick_from(parents, parents, labels)
    offsets = jnp.where(parents != labels, pick_from(counts, parents, labels), 0) + jnp.where(
        grands != parents, pick_from(counts, grands, labels), 0
    )
    tok_start = pick_from(starts, segments, labels)
    tok_offset = pick_from(offsets, segments, labels)
    tok_parent = pick_from(parents, segments, labels)
    tok_grand = pick_from(grands, segments, labels)
    positions = (places - tok_start + tok_offset).astype(jnp.float32)
    same_seg = (segments[None, :] == segments[:, None]) & (places[None, :] <= places[:, None])
    from_parent = (segments[None, :] == tok_parent[:, None]) & (tok_parent != segments)[:, None]
    from_grand = (segments[None, :] == tok_grand[:, None]) & (tok_grand != tok_parent)[:, None]
    visible = same_seg | from_parent | from_grand
    inv_freq = jnp.exp(
        jnp.arange(HEAD_WIDTH // 2, dtype=jnp.float32) * (-2.0 * math.log(10000.0) / HEAD_WIDTH)
    )
    angles = positions[:, None] * inv_freq[None, :]
    return (visible, jnp.cos(angles), jnp.sin(angles))


def apply_rotary(value_rows, cos_rows, sin_rows):
    half_size = value_rows.shape[-1] // 2
    front_half = value_rows[..., :half_size]
    back_half = value_rows[..., half_size:]
    return jnp.concatenate(
        [
            front_half * cos_rows - back_half * sin_rows,
            back_half * cos_rows + front_half * sin_rows,
        ],
        axis=-1,
    )


def rotate_back(value_rows, cos_rows, sin_rows):
    half_size = value_rows.shape[-1] // 2
    front_half = value_rows[..., :half_size]
    back_half = value_rows[..., half_size:]
    return jnp.concatenate(
        [
            front_half * cos_rows + back_half * sin_rows,
            back_half * cos_rows - front_half * sin_rows,
        ],
        axis=-1,
    )


def product(former, latter):
    return jnp.dot(former, latter, preferred_element_type=jnp.float32)


def select(onehot, stacked):
    return jnp.einsum("e,erc->rc", onehot, stacked, preferred_element_type=jnp.float32).astype(
        jnp.bfloat16
    )


def project(inputs, weight, shrink, expand):
    inner_rank = jnp.einsum("li,ri->lr", inputs, shrink, preferred_element_type=jnp.float32)
    return (product(inputs, weight) + product(inner_rank, expand.astype(jnp.float32)), inner_rank)


def project_back(inputs, inner_rank, upstream, weight, shrink, expand):
    grad_expand = jnp.einsum("lr,lo->ro", inner_rank, upstream, preferred_element_type=jnp.float32)
    grad_inner = jnp.einsum("lo,ro->lr", upstream, expand, preferred_element_type=jnp.float32)
    grad_shrink = jnp.einsum("lr,li->ri", grad_inner, inputs, preferred_element_type=jnp.float32)
    grad_inputs = jnp.einsum(
        "lo,io->li", upstream, weight, preferred_element_type=jnp.float32
    ) + product(grad_inner, shrink.astype(jnp.float32))
    return (grad_inputs, grad_shrink, grad_expand)


def score_block(query_rows, rotated_keys, visible):
    scores = jnp.einsum(
        "qngd,knd->ngqk", query_rows, rotated_keys, preferred_element_type=jnp.float32
    )
    bounded = jnp.tanh(scores / 50.0)
    masked = jnp.where(visible[None, None], 50.0 * bounded, -1e30)
    return (bounded, masked)


def activate(gate_in, up_in):
    return jax.nn.gelu(gate_in, approximate=True) * up_in


def on_device(
    layer_input,
    cotangent,
    norm_gains,
    w_query,
    w_key,
    w_value,
    w_output,
    w_gate,
    w_up,
    w_down,
    query_shrink,
    key_shrink,
    value_shrink,
    output_shrink,
    gate_shrink,
    up_shrink,
    down_shrink,
    query_expand,
    key_expand,
    value_expand,
    output_expand,
    gate_expand,
    up_expand,
    down_expand,
    adapter_ids,
    parent_segments,
    segment_ids,
):
    norm_gain = norm_gains.astype(jnp.float32)
    w_query, w_key, w_value, w_output, w_gate, w_up, w_down = (
        lax.all_gather(w_query, "dp", axis=0, tiled=True),
        lax.all_gather(w_key, "dp", axis=0, tiled=True),
        lax.all_gather(w_value, "dp", axis=0, tiled=True),
        lax.all_gather(w_output, "dp", axis=1, tiled=True),
        lax.all_gather(w_gate, "dp", axis=0, tiled=True),
        lax.all_gather(w_up, "dp", axis=0, tiled=True),
        lax.all_gather(w_down, "dp", axis=1, tiled=True),
    )
    labels = jnp.arange(ADAPTERS, dtype=jnp.int32)
    onehot = (labels == adapter_ids[0]).astype(jnp.bfloat16)
    chosen = [
        select(onehot, stacked)
        for stacked in (
            query_shrink,
            key_shrink,
            value_shrink,
            output_shrink,
            gate_shrink,
            up_shrink,
            down_shrink,
            query_expand,
            key_expand,
            value_expand,
            output_expand,
            gate_expand,
            up_expand,
            down_expand,
        )
    ]
    s_query, s_key, s_value, s_output, s_gate, s_up, s_down = chosen[:7]
    e_query, e_key, e_value, e_output, e_gate, e_up, e_down = chosen[7:]
    visible, cos_rows, sin_rows = tree_tables(segment_ids, parent_segments[0])
    cosine_per_head = cos_rows[:, None, :]
    sine_per_head = sin_rows[:, None, :]
    own_rows = layer_input.astype(jnp.float32)
    normed = rms_scale(own_rows, norm_gain[0]).astype(jnp.bfloat16)
    normed_all = lax.all_gather(normed, "tensor", axis=0, tiled=True)
    sequence_length = normed_all.shape[0]
    query_pre, query_inner = project(normed_all, w_query, s_query, e_query)
    key_before_rotation, key_inner = project(normed_all, w_key, s_key, e_key)
    value_projected, value_inner = project(normed_all, w_value, s_value, e_value)
    heads_q = query_pre.shape[1] // HEAD_WIDTH
    heads_kv = key_before_rotation.shape[1] // HEAD_WIDTH
    head_groups = heads_q // heads_kv
    query_rows = (
        (
            apply_rotary(
                query_pre.reshape(sequence_length, heads_q, HEAD_WIDTH),
                cosine_per_head,
                sine_per_head,
            )
            * HEAD_WIDTH ** (-0.5)
        )
        .astype(jnp.bfloat16)
        .reshape(sequence_length, heads_kv, head_groups, HEAD_WIDTH)
    )
    rotated_keys = apply_rotary(
        key_before_rotation.reshape(sequence_length, heads_kv, HEAD_WIDTH),
        cosine_per_head,
        sine_per_head,
    ).astype(jnp.bfloat16)
    value_rows = value_projected.astype(jnp.bfloat16).reshape(sequence_length, heads_kv, HEAD_WIDTH)
    bounded, masked = score_block(query_rows, rotated_keys, visible)
    row_max = jnp.max(masked, axis=-1, keepdims=True)
    exponent = jnp.exp(masked - row_max)
    row_total = jnp.sum(exponent, axis=-1, keepdims=True)
    log_total = row_max + jnp.log(row_total)
    probs_low = (exponent / row_total).astype(jnp.bfloat16)
    mixed_heads = (
        jnp.einsum("ngqk,knd->qngd", probs_low, value_rows, preferred_element_type=jnp.float32)
        .reshape(sequence_length, heads_q * HEAD_WIDTH)
        .astype(jnp.bfloat16)
    )
    attn_part, output_inner = project(mixed_heads, w_output, s_output, e_output)
    attended = lax.psum_scatter(
        attn_part.astype(jnp.bfloat16), "tensor", scatter_dimension=0, tiled=True
    ).astype(jnp.float32)
    residual = own_rows + rms_scale(attended, norm_gain[1])
    normed_ffn = rms_scale(residual, norm_gain[2]).astype(jnp.bfloat16)
    ffn_rows = lax.all_gather(normed_ffn, "tensor", axis=0, tiled=True)
    gate_pre, gate_inner = project(ffn_rows, w_gate, s_gate, e_gate)
    up_pre, up_inner = project(ffn_rows, w_up, s_up, e_up)
    hidden_full, act_back = jax.vjp(activate, gate_pre, up_pre)
    hidden = hidden_full.astype(jnp.bfloat16)
    ffn_part, down_inner = project(hidden, w_down, s_down, e_down)
    ffn_out = lax.psum_scatter(
        ffn_part.astype(jnp.bfloat16), "tensor", scatter_dimension=0, tiled=True
    ).astype(jnp.float32)
    layer_output = (residual + rms_scale(ffn_out, norm_gain[3])).astype(jnp.bfloat16)
    grad_out = cotangent.astype(jnp.float32)
    grad_ffn = rms_back(ffn_out, norm_gain[3], grad_out).astype(jnp.bfloat16)
    grad_ffn_all = lax.all_gather(grad_ffn, "tensor", axis=0, tiled=True)
    down_back = project_back(hidden, down_inner, grad_ffn_all, w_down, s_down, e_down)
    grad_gate, grad_up = act_back(down_back[0])
    grad_gate = grad_gate.astype(jnp.bfloat16)
    grad_up = grad_up.astype(jnp.bfloat16)
    gate_back = project_back(ffn_rows, gate_inner, grad_gate, w_gate, s_gate, e_gate)
    up_back = project_back(ffn_rows, up_inner, grad_up, w_up, s_up, e_up)
    grad_normed_ffn = lax.psum_scatter(
        (gate_back[0] + up_back[0]).astype(jnp.bfloat16), "tensor", scatter_dimension=0, tiled=True
    ).astype(jnp.float32)
    grad_resid = grad_out + rms_back(residual, norm_gain[2], grad_normed_ffn)
    grad_attn = rms_back(attended, norm_gain[1], grad_resid).astype(jnp.bfloat16)
    grad_attn_all = lax.all_gather(grad_attn, "tensor", axis=0, tiled=True)
    output_back = project_back(
        mixed_heads, output_inner, grad_attn_all, w_output, s_output, e_output
    )
    grad_mixed = (
        output_back[0]
        .astype(jnp.bfloat16)
        .reshape(sequence_length, heads_kv, head_groups, HEAD_WIDTH)
    )
    bounded, masked = score_block(query_rows, rotated_keys, visible)
    attn_probs = jnp.exp(masked - log_total)
    probs_low = attn_probs.astype(jnp.bfloat16)
    grad_values = (
        jnp.einsum("ngqk,qngd->knd", probs_low, grad_mixed, preferred_element_type=jnp.float32)
        .reshape(sequence_length, heads_kv * HEAD_WIDTH)
        .astype(jnp.bfloat16)
    )
    grad_probs = jnp.einsum(
        "qngd,knd->ngqk", grad_mixed, value_rows, preferred_element_type=jnp.float32
    )
    grad_capped = attn_probs * (
        grad_probs - jnp.sum(attn_probs * grad_probs, axis=-1, keepdims=True)
    )
    grad_scores = (grad_capped * (1.0 - bounded * bounded)).astype(jnp.bfloat16)
    grad_queries = jnp.einsum(
        "ngqk,knd->qngd", grad_scores, rotated_keys, preferred_element_type=jnp.float32
    ).reshape(sequence_length, heads_q, HEAD_WIDTH)
    grad_keys = jnp.einsum(
        "ngqk,qngd->knd", grad_scores, query_rows, preferred_element_type=jnp.float32
    )
    grad_qpre = (
        rotate_back(grad_queries * HEAD_WIDTH ** (-0.5), cosine_per_head, sine_per_head)
        .reshape(sequence_length, heads_q * HEAD_WIDTH)
        .astype(jnp.bfloat16)
    )
    grad_kpre = (
        rotate_back(grad_keys, cosine_per_head, sine_per_head)
        .reshape(sequence_length, heads_kv * HEAD_WIDTH)
        .astype(jnp.bfloat16)
    )
    query_back = project_back(normed_all, query_inner, grad_qpre, w_query, s_query, e_query)
    key_back = project_back(normed_all, key_inner, grad_kpre, w_key, s_key, e_key)
    value_back = project_back(normed_all, value_inner, grad_values, w_value, s_value, e_value)
    grad_normed = lax.psum_scatter(
        (query_back[0] + key_back[0] + value_back[0]).astype(jnp.bfloat16),
        "tensor",
        scatter_dimension=0,
        tiled=True,
    ).astype(jnp.float32)
    input_grad = grad_resid + rms_back(own_rows, norm_gain[0], grad_normed)
    hot_rows = onehot.astype(jnp.float32)[:, None, None]
    split_sums = (
        lax.psum((hot_rows * query_back[2][None]).astype(jnp.bfloat16), "dp").astype(jnp.float32),
        lax.psum((hot_rows * key_back[2][None]).astype(jnp.bfloat16), "dp").astype(jnp.float32),
        lax.psum((hot_rows * value_back[2][None]).astype(jnp.bfloat16), "dp").astype(jnp.float32),
        lax.psum((hot_rows * output_back[1][None]).astype(jnp.bfloat16), "dp").astype(jnp.float32),
        lax.psum((hot_rows * gate_back[2][None]).astype(jnp.bfloat16), "dp").astype(jnp.float32),
        lax.psum((hot_rows * up_back[2][None]).astype(jnp.bfloat16), "dp").astype(jnp.float32),
        lax.psum((hot_rows * down_back[1][None]).astype(jnp.bfloat16), "dp").astype(jnp.float32),
    )
    shared_sums = lax.psum(
        (
            hot_rows * query_back[1][None],
            hot_rows * key_back[1][None],
            hot_rows * value_back[1][None],
            hot_rows * output_back[2][None],
            hot_rows * gate_back[1][None],
            hot_rows * up_back[1][None],
            hot_rows * down_back[2][None],
        ),
        ("dp", "tensor"),
    )
    return (
        layer_output,
        input_grad,
        shared_sums[0],
        shared_sums[1],
        shared_sums[2],
        split_sums[3],
        shared_sums[4],
        shared_sums[5],
        split_sums[6],
        split_sums[0],
        split_sums[1],
        split_sums[2],
        shared_sums[3],
        split_sums[4],
        split_sums[5],
        shared_sums[6],
    )


def solution(mesh):
    placed = (
        P(("dp", "tensor"), None),
        P(("dp", "tensor"), None),
        P(),
        P("dp", "tensor"),
        P("dp", "tensor"),
        P("dp", "tensor"),
        P("tensor", "dp"),
        P("dp", "tensor"),
        P("dp", "tensor"),
        P("tensor", "dp"),
        P(),
        P(),
        P(),
        P(None, None, "tensor"),
        P(),
        P(),
        P(None, None, "tensor"),
        P(None, None, "tensor"),
        P(None, None, "tensor"),
        P(None, None, "tensor"),
        P(),
        P(None, None, "tensor"),
        P(None, None, "tensor"),
        P(),
        P("dp"),
        P("dp", None),
        P("dp"),
    )
    return jax.shard_map(
        on_device,
        mesh=mesh,
        in_specs=placed,
        out_specs=(
            P(("dp", "tensor"), None),
            P(("dp", "tensor"), None),
            P(),
            P(),
            P(),
            P(None, None, "tensor"),
            P(),
            P(),
            P(None, None, "tensor"),
            P(None, None, "tensor"),
            P(None, None, "tensor"),
            P(None, None, "tensor"),
            P(),
            P(None, None, "tensor"),
            P(None, None, "tensor"),
            P(),
        ),
        check_vma=False,
    )
```

profile of v0, /device:TPU:0, one launch (start us, length us, event | category | flops | bytes accessed | tf_op | source)
XLA Modules:
  0.0 1369.6 jit_solution(2153370588222020406)
XLA Ops:
  26.4 17.0 %all-gather.12.cloned.1.call-done = bf16[640,2304]{1,0:T(8,128)(2,1)} async-done(((bf16[160,2304]{1,0:T(8,128)(2,1)}), bf16[640,2304]{1,0:T(8,128)(2,1)}) %all-gather.12.cloned.1.call-update) | async-done | bytes 2949136 | tf_op jit(solution)/shard_map/all_gather | solution.py:187
  43.4 2.8 fusion.129
  46.2 51.4 %all-gather.18.cloned.1.call-done = bf16[2304,512]{1,0:T(8,128)(2,1)} async-done(((bf16[288,512]{1,0:T(8,128)(2,1)}), bf16[2304,512]{1,0:T(8,128)(2,1)}) %all-gather.18.cloned.1.call-update) | async-done | bytes 2359312 | tf_op jit(solution)/shard_map/all_gather | solution.py:151
  97.7 3.7 fusion.192
  109.0 30.4 %all-gather.16.cloned.1.call-done = bf16[2304,256]{1,0:T(8,128)(2,1)} async-done(((bf16[288,256]{1,0:T(8,128)(2,1)}), bf16[2304,256]{1,0:T(8,128)(2,1)}) %all-gather.16.cloned.1.call-update) | async-done | bytes 1179664 | tf_op jit(solution)/shard_map/all_gather | solution.py:152
  139.5 2.4 fusion.191
  143.9 37.5 %all-gather.14.cloned.1.call-done = bf16[2304,256]{1,0:T(8,128)(2,1)} async-done(((bf16[288,256]{1,0:T(8,128)(2,1)}), bf16[2304,256]{1,0:T(8,128)(2,1)}) %all-gather.14.cloned.1.call-update) | async-done | bytes 1179664 | tf_op jit(solution)/shard_map/all_gather | solution.py:153
  190.3 44.0 %all-gather.20.cloned.1.call-done = bf16[512,2304]{0,1:T(8,128)(2,1)} async-done(((bf16[512,288]{0,1:T(8,128)(2,1)}), bf16[512,2304]{0,1:T(8,128)(2,1)}) %all-gather.20.cloned.1.call-update) | async-done | bytes 2359312 | tf_op jit(solution)/shard_map/all_gather | solution.py:154
  234.3 3.4 fusion.193
  237.7 2.6 add_convert_fusion.3
  240.4 35.4 %reduce-scatter.5.cloned.1.call-done = bf16[160,2304]{1,0:T(8,128)(2,1)} async-done(((bf16[640,2304]{1,0:T(8,128)(2,1)}), bf16[160,2304]{1,0:T(8,128)(2,1)}) %reduce-scatter.5.cloned.1.call-update) | async-done | bytes 737296 | tf_op jit(solution)/shard_map/reduce_scatter | solution.py:225
  280.0 2.5 multiply_convert_fusion.2
  287.9 22.2 %all-gather.22.cloned.1.call-done = bf16[640,2304]{1,0:T(8,128)(2,1)} async-done(((bf16[160,2304]{1,0:T(8,128)(2,1)}), bf16[640,2304]{1,0:T(8,128)(2,1)}) %all-gather.22.cloned.1.call-update) | async-done | bytes 2949136 | tf_op jit(solution)/shard_map/all_gather | solution.py:230
  310.1 3.5 fusion.134
  313.5 2.4 fusion.132
  315.9 149.0 %all-gather.24.cloned.1.call-done = bf16[2304,2304]{1,0:T(8,128)(2,1)} async-done(((bf16[288,2304]{1,0:T(8,128)(2,1)}), bf16[2304,2304]{1,0:T(8,128)(2,1)}) %all-gather.24.cloned.1.call-update) | async-done | bytes 10616848 | tf_op jit(solution)/shard_map/all_gather | solution.py:155
  465.0 9.6 fusion.194
  474.5 3.4 convolution_add_fusion.2
  478.0 140.1 %all-gather.26.cloned.1.call-done = bf16[2304,2304]{1,0:T(8,128)(2,1)} async-done(((bf16[288,2304]{1,0:T(8,128)(2,1)}), bf16[2304,2304]{1,0:T(8,128)(2,1)}) %all-gather.26.cloned.1.call-update) | async-done | bytes 10616848 | tf_op jit(solution)/shard_map/all_gather | solution.py:156
  618.0 9.5 fusion.195
  627.6 4.2 multiply_convert_fusion.1
  634.9 136.1 %all-gather.28.cloned.1.call-done = bf16[2304,2304]{0,1:T(8,128)(2,1)} async-done(((bf16[2304,288]{0,1:T(8,128)(2,1)}), bf16[2304,2304]{0,1:T(8,128)(2,1)}) %all-gather.28.cloned.1.call-update) | async-done | bytes 10616848 | tf_op jit(solution)/shard_map/all_gather | solution.py:157
  771.0 10.4 fusion.196
  781.4 2.6 add_convert_fusion.2
  784.1 35.0 %reduce-scatter.7.cloned.1.call-done = bf16[160,2304]{1,0:T(8,128)(2,1)} async-done(((bf16[640,2304]{1,0:T(8,128)(2,1)}), bf16[160,2304]{1,0:T(8,128)(2,1)}) %reduce-scatter.7.cloned.1.call-update) | async-done | bytes 737296 | tf_op jit(solution)/shard_map/reduce_scatter | solution.py:236
  820.9 2.6 fusion.27
  823.6 27.5 %all-gather.30.cloned.1.call-done = bf16[640,2304]{1,0:T(8,128)(2,1)} async-done(((bf16[160,2304]{1,0:T(8,128)(2,1)}), bf16[640,2304]{1,0:T(8,128)(2,1)}) %all-gather.30.cloned.1.call-update) | async-done | bytes 2949136 | tf_op jit(solution)/shard_map/all_gather | solution.py:242
  851.1 11.4 fusion.197
  863.5 8.0 fusion.6
  874.5 12.2 fusion.199
  886.7 12.2 fusion.198
  898.8 7.3 add_convert_fusion.1
  906.7 36.3 %reduce-scatter.9.cloned.1.call-done = bf16[160,2304]{1,0:T(8,128)(2,1)} async-done(((bf16[640,2304]{1,0:T(8,128)(2,1)}), bf16[160,2304]{1,0:T(8,128)(2,1)}) %reduce-scatter.9.cloned.1.call-update) | async-done | bytes 737296 | tf_op jit(solution)/shard_map/reduce_scatter | solution.py:249
  945.2 4.2 fusion.33
  952.6 3.3 fusion.208
  961.7 17.8 %all-gather.32.cloned.1.call-done = bf16[640,2304]{1,0:T(8,128)(2,1)} async-done(((bf16[160,2304]{1,0:T(8,128)(2,1)}), bf16[640,2304]{1,0:T(8,128)(2,1)}) %all-gather.32.cloned.1.call-update) | async-done | bytes 2949136 | tf_op jit(solution)/shard_map/all_gather | solution.py:254
  979.5 2.8 fusion.130
  982.7 3.8 fusion.200
  1003.6 3.6 fusion.128
  1007.2 3.4 fusion.126
  1010.6 3.5 fusion.124
  1017.9 4.0 multiply_convert_fusion.3
  1026.7 10.2 add_convert_fusion
  1037.5 90.8 %all-reduce.7.cloned.1.call-done = (bf16[8,16,512]{2,1,0:T(8,128)(2,1)}, bf16[8,16,2304]{2,1,0:T(8,128)(2,1)}, bf16[8,16,512]{2,1,0:T(8,128)(2,1)}, bf16[8,16,25...) async-done(((bf16[8,16,512]{2,1,0:T(8,128)(2,1)}, bf16[8,16,2304]{2,1,0:T(8,128)(2,1)}, ...) | async-done | bytes 2162704 | tf_op jit(solution)/shard_map/psum | solution.py:309
  1139.2 27.3 %reduce-scatter.11.cloned.1.call-done = bf16[160,2304]{1,0:T(8,128)(2,1)} async-done(((bf16[640,2304]{1,0:T(8,128)(2,1)}), bf16[160,2304]{1,0:T(8,128)(2,1)}) %reduce-scatter.11.cloned.1.call-update) | async-done | bytes 737296 | tf_op jit(solution)/shard_map/reduce_scatter | solution.py:297
  1168.0 2.7 fusion.45
  1170.7 183.6 %all-reduce.5.cloned.1.call-done = (f32[8,16,2304]{2,1,0:T(8,128)}, f32[8,16,2304]{2,1,0:T(8,128)}, f32[8,16,2304]{2,1,0:T(8,128)}, f32[8,16,2304]{2,1,0:T(8,128...) async-done(((f32[8,16,2304]{2,1,0:T(8,128)}, f32[8,16,2304]{2,1,0:T(8,128)}, f32[8,16,2304]{2,1,0:T(8,128)}, f32[8,16,2304]{2,1,0:T(8,128)}, ...) | async-done | bytes 8257552 | tf_op jit(solution)/shard_map/psum | solution.py:314
  1354.2 2.5 copy.208
  (422 shorter events, 111.0 us)
Async XLA Ops:
  7.3 14.0 %copy-start.58 = (bf16[8,16,2304]{2,1,0:T(8,128)(2,1)S(1)}, bf16[8,16,2304]{2,1,0:T(8,128)(2,1)}, u32[]{:S(2)}) copy-start(bf16[8,16,2304]{2,1,0:T(8,128)(2,1)} %param.38) | copy-start | bytes 1769476
  7.3 15.0 %copy-start.59 = (bf16[8,16,2304]{2,1,0:T(8,128)(2,1)S(1)}, bf16[8,16,2304]{2,1,0:T(8,128)(2,1)}, u32[]{:S(2)}) copy-start(bf16[8,16,2304]{2,1,0:T(8,128)(2,1)} %param.39) | copy-start | bytes 1769476
  7.3 36.1 %all-gather.12.cloned.1.call-start = ((), (), s32[]{:S(2)}) async-start(), calls=%async_computation.4 | async-start | bytes 3686400 | tf_op jit(solution)/shard_map/all_gather | solution.py:187
  10.8 269.1 %copy-start.78 = (f32[2304]{0:T(1024)}, f32[2304]{0:T(1024)S(1)}, u32[]{:S(2)}) copy-start(f32[2304]{0:T(1024)S(1)} %get-tuple-element.20) | copy-start | bytes 27652
  13.1 84.6 %all-gather.18.cloned.1.call-start = ((), (), s32[]{:S(2)}) async-start(), calls=%async_computation.7 | async-start | bytes 2654208 | tf_op jit(solution)/shard_map/all_gather | solution.py:151
  13.9 125.6 %all-gather.16.cloned.1.call-start = ((), (), s32[]{:S(2)}) async-start(), calls=%async_computation.6 | async-start | bytes 1327104 | tf_op jit(solution)/shard_map/all_gather | solution.py:152
  14.6 166.8 %all-gather.14.cloned.1.call-start = ((), (), s32[]{:S(2)}) async-start(), calls=%async_computation.5 | async-start | bytes 1327104 | tf_op jit(solution)/shard_map/all_gather | solution.py:153
  15.2 219.1 %all-gather.20.cloned.1.call-start = ((), (), s32[]{:S(2)}) async-start(), calls=%async_computation.8 | async-start | bytes 2654208 | tf_op jit(solution)/shard_map/all_gather | solution.py:154
  15.8 260.0 %reduce-scatter.5.cloned.1.call-start = ((), (), s32[]{:S(2)}) async-start(), calls=%async_computation.9 | async-start | bytes 3686400 | tf_op jit(solution)/shard_map/reduce_scatter | solution.py:225
  17.1 166.9 %copy-start.112 = (f32[640]{0:T(1024)}, f32[640]{0:T(1024)S(1)}, u32[]{:S(2)}) copy-start(f32[640]{0:T(1024)S(1)} %add_convert_fusion.5) | copy-start | bytes 7684
  22.6 120.5 %copy-start.73 = (bf16[1,16,2304]{2,0,1:T(2,128)(2,1)}, bf16[1,16,2304]{2,0,1:T(2,128)(2,1)S(1)}, u32[]{:S(2)}) copy-start(bf16[1,16,2304]{2,0,1:T(2,128)(2,1)S(1)} %fusion.92) | copy-start | bytes 221188
  24.3 164.2 %copy-start.24 = (pred[640,640]{0,1:T(8,128)(4,1)}, pred[640,640]{0,1:T(8,128)(4,1)S(1)}, u32[]{:S(2)}) copy-start(pred[640,640]{0,1:T(8,128)(4,1)S(1)} %fusion.25) | copy-start | bytes 1228804
  43.4 54.3 %copy-start.2 = (bf16[640,2304]{1,0:T(8,128)(2,1)S(1)}, bf16[640,2304]{1,0:T(8,128)(2,1)}, u32[]{:S(2)}) copy-start(bf16[640,2304]{1,0:T(8,128)(2,1)} %all-gather.12.cloned.1.call-done) | copy-start | bytes 8847364
  46.2 55.2 %copy-start.92 = (bf16[640,16]{0,1:T(8,128)(2,1)}, bf16[640,16]{0,1:T(8,128)(2,1)S(1)}, u32[]{:S(2)}) copy-start(bf16[640,16]{0,1:T(8,128)(2,1)S(1)} %fusion.129) | copy-start | bytes 61444
  109.0 32.9 %copy-start.103 = (bf16[640,16]{0,1:T(8,128)(2,1)}, bf16[640,16]{0,1:T(8,128)(2,1)S(1)}, u32[]{:S(2)}) copy-start(bf16[640,16]{0,1:T(8,128)(2,1)S(1)} %fusion.127) | copy-start | bytes 61444
  143.9 39.8 %copy-start.90 = (bf16[640,16]{0,1:T(8,128)(2,1)}, bf16[640,16]{0,1:T(8,128)(2,1)S(1)}, u32[]{:S(2)}) copy-start(bf16[640,16]{0,1:T(8,128)(2,1)S(1)} %fusion.125) | copy-start | bytes 61444
  143.9 39.9 %copy-start.114 = (bf16[1,16,256]{2,0,1:T(2,128)(2,1)S(1)}, bf16[1,16,256]{2,0,1:T(2,128)(2,1)}, u32[]{:S(2)}) copy-start(bf16[1,16,256]{2,0,1:T(2,128)(2,1)} %fusion.122) | copy-start | bytes 24580
  143.9 40.2 %copy-start.135 = (f32[128]{0:T(128)S(1)}, f32[128]{0:T(128)}, u32[]{:S(2)}) copy-start(f32[128]{0:T(128)} %copy-done.134) | copy-start | bytes 1540
  190.0 47.7 %copy-start.22 = (bf16[256,2,640]{2,0,1:T(8,128)(2,1)}, bf16[256,2,640]{2,0,1:T(8,128)(2,1)S(1)}, u32[]{:S(2)}) copy-start(bf16[256,2,640]{2,0,1:T(8,128)(2,1)S(1)} %fusion.54) | copy-start | bytes 1966084
  190.3 47.5 %copy-start.99 = (bf16[640,16]{0,1:T(8,128)(2,1)}, bf16[640,16]{0,1:T(8,128)(2,1)S(1)}, u32[]{:S(2)}) copy-start(bf16[640,16]{0,1:T(8,128)(2,1)S(1)} %fusion.141) | copy-start | bytes 61444
  190.3 47.5 %copy-start.54 = (bf16[1,16,2304]{2,0,1:T(2,128)(2,1)S(1)}, bf16[1,16,2304]{2,0,1:T(2,128)(2,1)}, u32[]{:S(2)}) copy-start(bf16[1,16,2304]{2,0,1:T(2,128)(2,1)} %fusion.86) | copy-start | bytes 221188
  240.3 37.4 %copy-start.5 = (bf16[160,2304]{1,0:T(8,128)(2,1)S(1)}, bf16[160,2304]{1,0:T(8,128)(2,1)}, u32[]{:S(2)}) copy-start(bf16[160,2304]{1,0:T(8,128)(2,1)} %param.27) | copy-start | bytes 2211844
  240.3 39.6 %copy-start.97 = (f32[2304]{0:T(1024)S(1)}, f32[2304]{0:T(1024)}, u32[]{:S(2)}) copy-start(f32[2304]{0:T(1024)} %get-tuple-element.19) | copy-start | bytes 27652
  240.4 69.7 %all-gather.22.cloned.1.call-start = ((), (), s32[]{:S(2)}) async-start(), calls=%async_computation.10 | async-start | bytes 3686400 | tf_op jit(solution)/shard_map/all_gather | solution.py:230
  282.5 182.5 %all-gather.24.cloned.1.call-start = ((), (), s32[]{:S(2)}) async-start(), calls=%async_computation.11 | async-start | bytes 11943936 | tf_op jit(solution)/shard_map/all_gather | solution.py:155
  283.3 334.8 %all-gather.26.cloned.1.call-start = ((), (), s32[]{:S(2)}) async-start(), calls=%async_computation.12 | async-start | bytes 11943936 | tf_op jit(solution)/shard_map/all_gather | solution.py:156
  284.0 487.0 %all-gather.28.cloned.1.call-start = ((), (), s32[]{:S(2)}) async-start(), calls=%async_computation.13 | async-start | bytes 11943936 | tf_op jit(solution)/shard_map/all_gather | solution.py:157
  284.6 534.6 %reduce-scatter.7.cloned.1.call-start = ((), (), s32[]{:S(2)}) async-start(), calls=%async_computation.14 | async-start | bytes 3686400 | tf_op jit(solution)/shard_map/reduce_scatter | solution.py:236
  784.0 35.1 %copy-start.96 = (f32[2304]{0:T(1024)S(1)}, f32[2304]{0:T(1024)}, u32[]{:S(2)}) copy-start(f32[2304]{0:T(1024)} %get-tuple-element.18) | copy-start | bytes 27652
  784.1 67.1 %all-gather.30.cloned.1.call-start = ((), (), s32[]{:S(2)}) async-start(), calls=%async_computation.15 | async-start | bytes 3686400 | tf_op jit(solution)/shard_map/all_gather | solution.py:242
  823.6 119.5 %reduce-scatter.9.cloned.1.call-start = ((), (), s32[]{:S(2)}) async-start(), calls=%async_computation.16 | async-start | bytes 3686400 | tf_op jit(solution)/shard_map/reduce_scatter | solution.py:249
  871.5 15.2 %copy-start.15 = (bf16[640,2304]{1,0:T(8,128)(2,1)}, bf16[640,2304]{1,0:T(8,128)(2,1)S(1)}, u32[]{:S(2)}) copy-start(bf16[640,2304]{1,0:T(8,128)(2,1)S(1)} %get-tuple-element.46) | copy-start | bytes 8847364
  906.1 36.9 %copy-start.79 = (f32[2304]{0:T(1024)S(1)}, f32[2304]{0:T(1024)}, u32[]{:S(2)}) copy-start(f32[2304]{0:T(1024)} %copy-done.78) | copy-start | bytes 27652
  906.2 36.9 %copy-start.98 = (f32[2304]{0:T(1024)S(1)}, f32[2304]{0:T(1024)}, u32[]{:S(2)}) copy-start(f32[2304]{0:T(1024)} %get-tuple-element.19) | copy-start | bytes 27652
  906.2 36.9 %copy-start.121 = (f32[160]{0:T(256)S(1)}, f32[160]{0:T(256)}, u32[]{:S(2)}) copy-start(f32[160]{0:T(256)} %copy-done.120) | copy-start | bytes 1924
  906.2 39.0 %copy-start.130 = (f32[160]{0:T(256)S(1)}, f32[160]{0:T(256)}, u32[]{:S(2)}) copy-start(f32[160]{0:T(256)} %copy-done.129) | copy-start | bytes 1924
  906.2 39.0 %copy-start.140 = (f32[160]{0:T(256)S(1)}, f32[160]{0:T(256)}, u32[]{:S(2)}) copy-start(f32[160]{0:T(256)} %get-tuple-element.67) | copy-start | bytes 1924
  906.2 73.3 %all-gather.32.cloned.1.call-start = ((), (), s32[]{:S(2)}) async-start(), calls=%async_computation.17 | async-start | bytes 3686400 | tf_op jit(solution)/shard_map/all_gather | solution.py:254
  951.9 176.5 %all-reduce.7.cloned.1.call-start = ((), (), s32[]{:S(2)}) async-start(), calls=%async_computation.20 | async-start | bytes 4325376 | tf_op jit(solution)/shard_map/psum | solution.py:309
  952.5 34.4 %copy-start.126 = (f32[2,640]{1,0:T(2,128)}, f32[2,640]{1,0:T(2,128)S(1)}, u32[]{:S(2)}) copy-start(f32[2,640]{1,0:T(2,128)S(1)} %log_add_fusion) | copy-start | bytes 15364
  959.4 20.1 %copy-start.55 = (bf16[1,16,2304]{2,0,1:T(2,128)(2,1)S(1)}, bf16[1,16,2304]{2,0,1:T(2,128)(2,1)}, u32[]{:S(2)}) copy-start(bf16[1,16,2304]{2,0,1:T(2,128)(2,1)} %fusion.86) | copy-start | bytes 221188
  1021.9 144.6 %reduce-scatter.11.cloned.1.call-start = ((), (), s32[]{:S(2)}) async-start(), calls=%async_computation.18 | async-start | bytes 3686400 | tf_op jit(solution)/shard_map/reduce_scatter | solution.py:297
  1036.9 317.3 %all-reduce.5.cloned.1.call-start = ((), (), s32[]{:S(2)}) async-start(), calls=%async_computation.19 | async-start | bytes 16515072 | tf_op jit(solution)/shard_map/psum | solution.py:314
  1131.6 35.0 %copy-start.6 = (bf16[160,2304]{1,0:T(8,128)(2,1)S(1)}, bf16[160,2304]{1,0:T(8,128)(2,1)}, u32[]{:S(2)}) copy-start(bf16[160,2304]{1,0:T(8,128)(2,1)} %param.27) | copy-start | bytes 2211844
  1131.6 35.0 %copy-start.95 = (f32[2304]{0:T(1024)S(1)}, f32[2304]{0:T(1024)}, u32[]{:S(2)}) copy-start(f32[2304]{0:T(1024)} %copy-done.94) | copy-start | bytes 27652
  1137.0 31.0 %copy-start.18 = (f32[160,2304]{1,0:T(8,128)S(1)}, f32[160,2304]{1,0:T(8,128)}, u32[]{:S(2)}) copy-start(f32[160,2304]{1,0:T(8,128)} %copy-done.17) | copy-start | bytes 4423684
  1137.0 31.0 %copy-start.132 = (f32[160]{0:T(256)S(1)}, f32[160]{0:T(256)}, u32[]{:S(2)}) copy-start(f32[160]{0:T(256)} %copy-done.131) | copy-start | bytes 1924
  1137.0 31.0 %copy-start.139 = (f32[160]{0:T(256)S(1)}, f32[160]{0:T(256)}, u32[]{:S(2)}) copy-start(f32[160]{0:T(256)} %get-tuple-element.63) | copy-start | bytes 1924
  (110 other events, 459.9 us)
Sparse Core Ops, SparseCore 0:
  13.2 30.1 all-gather.11
  45.6 52.0 all-gather.17
  99.9 39.5 all-gather.15
  141.5 39.8 all-gather.13
  183.4 50.8 all-gather.19
  240.5 35.2 reduce-scatter.4
  282.6 27.4 all-gather.21
  312.5 152.4 all-gather.23
  467.4 150.6 all-gather.25
  620.3 150.6 all-gather.27
  784.2 34.9 reduce-scatter.6
  823.7 27.4 all-gather.29
  906.3 36.6 reduce-scatter.8
  952.0 27.4 all-gather.31
  1022.0 106.2 all-reduce.6
  1130.9 35.5 reduce-scatter.10
  1173.9 180.2 all-reduce.4
where the time goes:
time: 1380 us; the launch traced here: 1370 us
  waiting for transfers between devices  1090 us (79%)
  matrix products  187 us (14%)
  other arithmetic  55.4 us (4%)
  local copies, waits for them, and re-layouts  22.7 us (2%)
  between operations  16.2 us (1%)
    psum x1, waiting for transfers between devices, on_device(): lax.psum((hot_rows * query_back[1][None], hot_rows * key_back[1][None], h...  184 us
    all_gather x1, waiting for transfers between devices, on_device(): lax.all_gather(w_gate, 'dp', axis=0, tiled=True)  149 us
    all_gather x1, waiting for transfers between devices, on_device(): lax.all_gather(w_up, 'dp', axis=0, tiled=True)  140 us
    all_gather x1, waiting for transfers between devices, on_device(): lax.all_gather(w_down, 'dp', axis=1, tiled=True)  136 us
    psum x1, waiting for transfers between devices, on_device(): lax.psum((hot_rows * output_back[1][None]).astype(jnp.bfloat16), 'dp')  90.8 us
    dot_general x21, matrix products, product(): return jnp.dot(former, latter, preferred_element_type=jnp.float32)  83.2 us
    dot_general x7, matrix products, project_back(): jnp.einsum('lo,io->li', upstream, weight, preferred_element_type=jnp.floa...  52.5 us
    all_gather x1, waiting for transfers between devices, on_device(): lax.all_gather(w_query, 'dp', axis=0, tiled=True)  51.4 us
  transfers between devices with their start and end apart: 17, of which 17 were waited for; matrix products, arithmetic and copies ran while one was open for 8% of the time, Pallas kernels for 0%

commit v1 on v0

--- a/solution.py
+++ b/solution.py
@@ -312,16 +312,19 @@
         lax.psum((hot_rows * down_back[1][None]).astype(jnp.bfloat16), "dp").astype(jnp.float32),
     )
     shared_sums = lax.psum(
-        (
-            hot_rows * query_back[1][None],
-            hot_rows * key_back[1][None],
-            hot_rows * value_back[1][None],
-            hot_rows * output_back[2][None],
-            hot_rows * gate_back[1][None],
-            hot_rows * up_back[1][None],
-            hot_rows * down_back[2][None],
+        lax.psum(
+            (
+                hot_rows * query_back[1][None],
+                hot_rows * key_back[1][None],
+                hot_rows * value_back[1][None],
+                hot_rows * output_back[2][None],
+                hot_rows * gate_back[1][None],
+                hot_rows * up_back[1][None],
+                hot_rows * down_back[2][None],
+            ),
+            "tensor",
         ),
-        ("dp", "tensor"),
+        "dp",
     )
     return (
         layer_output,

time: 1380 us -> 1610 us (1.17)
  waiting for transfers between devices: 1090 us -> 1320 us
    psum x0 -> x1, waiting for transfers between devices: none -> 272 us  [on_device(): lax.psum(lax.psum((hot_rows * query_back[1][None], hot_rows * key_back[1]...]
    psum x1, waiting for transfers between devices: 184 us -> 125 us  [on_device(): lax.psum((hot_rows * query_back[1][None], hot_rows * key_back[1][None], h...]
    psum x1, waiting for transfers between devices: 90.8 us -> 112 us  [on_device(): lax.psum((hot_rows * output_back[1][None]).astype(jnp.bfloat16), 'dp')]
  transfers between devices with their start and end apart: 17 -> 18, of which waited for: 17 -> 18; matrix products, arithmetic and copies ran while one was open for 8% -> 8% of each run, Pallas kernels for 0% -> 0%
where the time goes in v1:
time: 1610 us; the launch traced here: 1600 us
  waiting for transfers between devices  1320 us (82%)
  matrix products  185 us (11%)
  other arithmetic  54.8 us (3%)
  local copies, waits for them, and re-layouts  23.2 us (1%)
  between operations  16.6 us (1%)
    psum x1, waiting for transfers between devices, on_device(): lax.psum(lax.psum((hot_rows * query_back[1][None], hot_rows * key_back[1]...  272 us
    all_gather x1, waiting for transfers between devices, on_device(): lax.all_gather(w_gate, 'dp', axis=0, tiled=True)  149 us
    all_gather x1, waiting for transfers between devices, on_device(): lax.all_gather(w_up, 'dp', axis=0, tiled=True)  140 us
    all_gather x1, waiting for transfers between devices, on_device(): lax.all_gather(w_down, 'dp', axis=1, tiled=True)  136 us
    psum x1, waiting for transfers between devices, on_device(): lax.psum((hot_rows * query_back[1][None], hot_rows * key_back[1][None], h...  125 us
    psum x1, waiting for transfers between devices, on_device(): lax.psum((hot_rows * output_back[1][None]).astype(jnp.bfloat16), 'dp')  112 us
    dot_general x21, matrix products, product(): return jnp.dot(former, latter, preferred_element_type=jnp.float32)  83.4 us
    dot_general x7, matrix products, project_back(): jnp.einsum('lo,io->li', upstream, weight, preferred_element_type=jnp.floa...  53 us
  transfers between devices with their start and end apart: 18, of which 18 were waited for; matrix products, arithmetic and copies ran while one was open for 8% of the time, Pallas kernels for 0%

profile of v1, /device:TPU:0, one launch (start us, length us, event | category | flops | bytes accessed | tf_op | source)
XLA Modules:
  0.0 1602.5 jit_solution(4788854369768272599)
XLA Ops:
  26.3 17.0 %all-gather.12.cloned.1.call-done = bf16[640,2304]{1,0:T(8,128)(2,1)} async-done(((bf16[160,2304]{1,0:T(8,128)(2,1)}), bf16[640,2304]{1,0:T(8,128)(2,1)}) %all-gather.12.cloned.1.call-update) | async-done | bytes 2949136 | tf_op jit(solution)/shard_map/all_gather | solution.py:187
  43.4 2.8 fusion.129
  46.2 51.4 %all-gather.18.cloned.1.call-done = bf16[2304,512]{1,0:T(8,128)(2,1)} async-done(((bf16[288,512]{1,0:T(8,128)(2,1)}), bf16[2304,512]{1,0:T(8,128)(2,1)}) %all-gather.18.cloned.1.call-update) | async-done | bytes 2359312 | tf_op jit(solution)/shard_map/all_gather | solution.py:151
  97.7 3.7 fusion.192
  109.0 30.5 %all-gather.16.cloned.1.call-done = bf16[2304,256]{1,0:T(8,128)(2,1)} async-done(((bf16[288,256]{1,0:T(8,128)(2,1)}), bf16[2304,256]{1,0:T(8,128)(2,1)}) %all-gather.16.cloned.1.call-update) | async-done | bytes 1179664 | tf_op jit(solution)/shard_map/all_gather | solution.py:152
  139.5 2.4 fusion.191
  143.9 37.5 %all-gather.14.cloned.1.call-done = bf16[2304,256]{1,0:T(8,128)(2,1)} async-done(((bf16[288,256]{1,0:T(8,128)(2,1)}), bf16[2304,256]{1,0:T(8,128)(2,1)}) %all-gather.14.cloned.1.call-update) | async-done | bytes 1179664 | tf_op jit(solution)/shard_map/all_gather | solution.py:153
  190.3 44.0 %all-gather.20.cloned.1.call-done = bf16[512,2304]{0,1:T(8,128)(2,1)} async-done(((bf16[512,288]{0,1:T(8,128)(2,1)}), bf16[512,2304]{0,1:T(8,128)(2,1)}) %all-gather.20.cloned.1.call-update) | async-done | bytes 2359312 | tf_op jit(solution)/shard_map/all_gather | solution.py:154
  234.3 3.4 fusion.193
  237.7 2.6 add_convert_fusion.3
  240.4 35.4 %reduce-scatter.5.cloned.1.call-done = bf16[160,2304]{1,0:T(8,128)(2,1)} async-done(((bf16[640,2304]{1,0:T(8,128)(2,1)}), bf16[160,2304]{1,0:T(8,128)(2,1)}) %reduce-scatter.5.cloned.1.call-update) | async-done | bytes 737296 | tf_op jit(solution)/shard_map/reduce_scatter | solution.py:225
  279.9 2.5 multiply_convert_fusion.2
  287.8 22.2 %all-gather.22.cloned.1.call-done = bf16[640,2304]{1,0:T(8,128)(2,1)} async-done(((bf16[160,2304]{1,0:T(8,128)(2,1)}), bf16[640,2304]{1,0:T(8,128)(2,1)}) %all-gather.22.cloned.1.call-update) | async-done | bytes 2949136 | tf_op jit(solution)/shard_map/all_gather | solution.py:230
  310.0 3.5 fusion.134
  313.5 2.4 fusion.132
  315.9 149.0 %all-gather.24.cloned.1.call-done = bf16[2304,2304]{1,0:T(8,128)(2,1)} async-done(((bf16[288,2304]{1,0:T(8,128)(2,1)}), bf16[2304,2304]{1,0:T(8,128)(2,1)}) %all-gather.24.cloned.1.call-update) | async-done | bytes 10616848 | tf_op jit(solution)/shard_map/all_gather | solution.py:155
  464.9 9.6 fusion.194
  474.5 3.4 convolution_add_fusion.2
  477.9 140.1 %all-gather.26.cloned.1.call-done = bf16[2304,2304]{1,0:T(8,128)(2,1)} async-done(((bf16[288,2304]{1,0:T(8,128)(2,1)}), bf16[2304,2304]{1,0:T(8,128)(2,1)}) %all-gather.26.cloned.1.call-update) | async-done | bytes 10616848 | tf_op jit(solution)/shard_map/all_gather | solution.py:156
  618.0 9.5 fusion.195
  627.6 4.2 multiply_convert_fusion.1
  634.8 136.1 %all-gather.28.cloned.1.call-done = bf16[2304,2304]{0,1:T(8,128)(2,1)} async-done(((bf16[2304,288]{0,1:T(8,128)(2,1)}), bf16[2304,2304]{0,1:T(8,128)(2,1)}) %all-gather.28.cloned.1.call-update) | async-done | bytes 10616848 | tf_op jit(solution)/shard_map/all_gather | solution.py:157
  770.9 10.4 fusion.196
  781.3 2.6 add_convert_fusion.2
  784.1 35.0 %reduce-scatter.7.cloned.1.call-done = bf16[160,2304]{1,0:T(8,128)(2,1)} async-done(((bf16[640,2304]{1,0:T(8,128)(2,1)}), bf16[160,2304]{1,0:T(8,128)(2,1)}) %reduce-scatter.7.cloned.1.call-update) | async-done | bytes 737296 | tf_op jit(solution)/shard_map/reduce_scatter | solution.py:236
  820.9 2.6 fusion.27
  823.5 27.5 %all-gather.30.cloned.1.call-done = bf16[640,2304]{1,0:T(8,128)(2,1)} async-done(((bf16[160,2304]{1,0:T(8,128)(2,1)}), bf16[640,2304]{1,0:T(8,128)(2,1)}) %all-gather.30.cloned.1.call-update) | async-done | bytes 2949136 | tf_op jit(solution)/shard_map/all_gather | solution.py:242
  851.1 11.4 fusion.197
  863.4 8.0 fusion.6
  874.4 12.2 fusion.199
  886.6 12.1 fusion.198
  898.7 7.3 add_convert_fusion.1
  906.6 36.4 %reduce-scatter.9.cloned.1.call-done = bf16[160,2304]{1,0:T(8,128)(2,1)} async-done(((bf16[640,2304]{1,0:T(8,128)(2,1)}), bf16[160,2304]{1,0:T(8,128)(2,1)}) %reduce-scatter.9.cloned.1.call-update) | async-done | bytes 737296 | tf_op jit(solution)/shard_map/reduce_scatter | solution.py:249
  945.2 4.2 fusion.33
  952.0 3.1 fusion.208
  961.0 18.4 %all-gather.32.cloned.1.call-done = bf16[640,2304]{1,0:T(8,128)(2,1)} async-done(((bf16[160,2304]{1,0:T(8,128)(2,1)}), bf16[640,2304]{1,0:T(8,128)(2,1)}) %all-gather.32.cloned.1.call-update) | async-done | bytes 2949136 | tf_op jit(solution)/shard_map/all_gather | solution.py:254
  979.4 4.7 fusion.200
  1003.3 4.0 multiply_convert_fusion.3
  1010.7 3.7 fusion.128
  1014.4 3.6 fusion.126
  1018.0 3.5 fusion.124
  1025.1 9.9 add_convert_fusion
  1035.0 125.4 %all-reduce.9.cloned.1.call-done = (f32[8,16,2304]{2,1,0:T(8,128)}, f32[8,16,2304]{2,1,0:T(8,128)}, f32[8,16,2304]{2,1,0:T(8,128)}, f32[8,16,2304]{2,1,0:T(8,128...) async-done(((f32[8,16,2304]{2,1,0:T(8,128)}, f32[8,16,2304]{2,1,0:T(8,128)}, f32[8,16,2304]{2,1,0:T(8,128)}, f32[8,16,2304]{2,1,0:T(8,128)}, ...) | async-done | bytes 8257552 | tf_op jit(solution)/shard_map/psum | solution.py:315
  1160.4 111.9 %all-reduce.11.cloned.1.call-done = (bf16[8,16,512]{2,1,0:T(8,128)(2,1)}, bf16[8,16,2304]{2,1,0:T(8,128)(2,1)}, bf16[8,16,512]{2,1,0:T(8,128)(2,1)}, bf16[8,16,2...) async-done(((bf16[8,16,512]{2,1,0:T(8,128)(2,1)}, bf16[8,16,2304]{2,1,0:T(8,128)(2,1)}, ...) | async-done | bytes 2162704 | tf_op jit(solution)/shard_map/psum | solution.py:309
  1283.1 27.2 %reduce-scatter.11.cloned.1.call-done = bf16[160,2304]{1,0:T(8,128)(2,1)} async-done(((bf16[640,2304]{1,0:T(8,128)(2,1)}), bf16[160,2304]{1,0:T(8,128)(2,1)}) %reduce-scatter.11.cloned.1.call-update) | async-done | bytes 737296 | tf_op jit(solution)/shard_map/reduce_scatter | solution.py:297
  1311.8 2.7 fusion.45
  1314.4 272.4 %all-reduce.7.cloned.1.call-done = (f32[8,16,2304]{2,1,0:T(8,128)}, f32[8,16,2304]{2,1,0:T(8,128)}, f32[8,16,2304]{2,1,0:T(8,128)}, f32[8,16,2304]{2,1,0:T(8,128...) async-done(((f32[8,16,2304]{2,1,0:T(8,128)}, f32[8,16,2304]{2,1,0:T(8,128)}, f32[8,16,2304]{2,1,0:T(8,128)}, f32[8,16,2304]{2,1,0:T(8,128)}, ...) | async-done | bytes 8257552 | tf_op jit(solution)/shard_map/psum | solution.py:314
  1586.8 2.5 copy.215
  (421 shorter events, 109.9 us)
Async XLA Ops:
  7.3 14.0 copy-start.58
  7.3 15.0 copy-start.59
  7.3 36.1 %all-gather.12.cloned.1.call-start = ((), (), s32[]{:S(2)}) async-start(), calls=%async_computation.4 | async-start | bytes 3686400 | tf_op jit(solution)/shard_map/all_gather | solution.py:187
  10.8 269.1 %copy-start.78 = (f32[2304]{0:T(1024)}, f32[2304]{0:T(1024)S(1)}, u32[]{:S(2)}) copy-start(f32[2304]{0:T(1024)S(1)} %get-tuple-element.20) | copy-start | bytes 27652
  13.1 84.6 %all-gather.18.cloned.1.call-start = ((), (), s32[]{:S(2)}) async-start(), calls=%async_computation.7 | async-start | bytes 2654208 | tf_op jit(solution)/shard_map/all_gather | solution.py:151
  13.8 125.7 %all-gather.16.cloned.1.call-start = ((), (), s32[]{:S(2)}) async-start(), calls=%async_computation.6 | async-start | bytes 1327104 | tf_op jit(solution)/shard_map/all_gather | solution.py:152
  14.6 166.8 %all-gather.14.cloned.1.call-start = ((), (), s32[]{:S(2)}) async-start(), calls=%async_computation.5 | async-start | bytes 1327104 | tf_op jit(solution)/shard_map/all_gather | solution.py:153
  15.2 219.1 %all-gather.20.cloned.1.call-start = ((), (), s32[]{:S(2)}) async-start(), calls=%async_computation.8 | async-start | bytes 2654208 | tf_op jit(solution)/shard_map/all_gather | solution.py:154
  15.7 260.0 %reduce-scatter.5.cloned.1.call-start = ((), (), s32[]{:S(2)}) async-start(), calls=%async_computation.9 | async-start | bytes 3686400 | tf_op jit(solution)/shard_map/reduce_scatter | solution.py:225
  17.1 167.0 %copy-start.114 = (f32[640]{0:T(1024)}, f32[640]{0:T(1024)S(1)}, u32[]{:S(2)}) copy-start(f32[640]{0:T(1024)S(1)} %add_convert_fusion.5) | copy-start | bytes 7684
  22.6 120.5 %copy-start.73 = (bf16[1,16,2304]{2,0,1:T(2,128)(2,1)}, bf16[1,16,2304]{2,0,1:T(2,128)(2,1)S(1)}, u32[]{:S(2)}) copy-start(bf16[1,16,2304]{2,0,1:T(2,128)(2,1)S(1)} %fusion.92) | copy-start | bytes 221188
  24.3 164.3 %copy-start.24 = (pred[640,640]{0,1:T(8,128)(4,1)}, pred[640,640]{0,1:T(8,128)(4,1)S(1)}, u32[]{:S(2)}) copy-start(pred[640,640]{0,1:T(8,128)(4,1)S(1)} %fusion.25) | copy-start | bytes 1228804
  43.4 54.3 %copy-start.2 = (bf16[640,2304]{1,0:T(8,128)(2,1)S(1)}, bf16[640,2304]{1,0:T(8,128)(2,1)}, u32[]{:S(2)}) copy-start(bf16[640,2304]{1,0:T(8,128)(2,1)} %all-gather.12.cloned.1.call-done) | copy-start | bytes 8847364
  46.2 55.2 %copy-start.92 = (bf16[640,16]{0,1:T(8,128)(2,1)}, bf16[640,16]{0,1:T(8,128)(2,1)S(1)}, u32[]{:S(2)}) copy-start(bf16[640,16]{0,1:T(8,128)(2,1)S(1)} %fusion.129) | copy-start | bytes 61444
  109.0 32.9 %copy-start.103 = (bf16[640,16]{0,1:T(8,128)(2,1)}, bf16[640,16]{0,1:T(8,128)(2,1)S(1)}, u32[]{:S(2)}) copy-start(bf16[640,16]{0,1:T(8,128)(2,1)S(1)} %fusion.127) | copy-start | bytes 61444
  143.9 39.8 %copy-start.90 = (bf16[640,16]{0,1:T(8,128)(2,1)}, bf16[640,16]{0,1:T(8,128)(2,1)S(1)}, u32[]{:S(2)}) copy-start(bf16[640,16]{0,1:T(8,128)(2,1)S(1)} %fusion.125) | copy-start | bytes 61444
  143.9 39.9 %copy-start.116 = (bf16[1,16,256]{2,0,1:T(2,128)(2,1)S(1)}, bf16[1,16,256]{2,0,1:T(2,128)(2,1)}, u32[]{:S(2)}) copy-start(bf16[1,16,256]{2,0,1:T(2,128)(2,1)} %fusion.122) | copy-start | bytes 24580
  143.9 40.2 %copy-start.134 = (f32[128]{0:T(128)S(1)}, f32[128]{0:T(128)}, u32[]{:S(2)}) copy-start(f32[128]{0:T(128)} %copy-done.133) | copy-start | bytes 1540
  190.0 47.7 %copy-start.22 = (bf16[256,2,640]{2,0,1:T(8,128)(2,1)}, bf16[256,2,640]{2,0,1:T(8,128)(2,1)S(1)}, u32[]{:S(2)}) copy-start(bf16[256,2,640]{2,0,1:T(8,128)(2,1)S(1)} %fusion.54) | copy-start | bytes 1966084
  190.2 47.5 %copy-start.99 = (bf16[640,16]{0,1:T(8,128)(2,1)}, bf16[640,16]{0,1:T(8,128)(2,1)S(1)}, u32[]{:S(2)}) copy-start(bf16[640,16]{0,1:T(8,128)(2,1)S(1)} %fusion.141) | copy-start | bytes 61444
  190.2 47.5 %copy-start.54 = (bf16[1,16,2304]{2,0,1:T(2,128)(2,1)S(1)}, bf16[1,16,2304]{2,0,1:T(2,128)(2,1)}, u32[]{:S(2)}) copy-start(bf16[1,16,2304]{2,0,1:T(2,128)(2,1)} %fusion.86) | copy-start | bytes 221188
  240.3 37.4 %copy-start.5 = (bf16[160,2304]{1,0:T(8,128)(2,1)S(1)}, bf16[160,2304]{1,0:T(8,128)(2,1)}, u32[]{:S(2)}) copy-start(bf16[160,2304]{1,0:T(8,128)(2,1)} %param.27) | copy-start | bytes 2211844
  240.3 39.6 %copy-start.97 = (f32[2304]{0:T(1024)S(1)}, f32[2304]{0:T(1024)}, u32[]{:S(2)}) copy-start(f32[2304]{0:T(1024)} %get-tuple-element.19) | copy-start | bytes 27652
  240.4 69.6 %all-gather.22.cloned.1.call-start = ((), (), s32[]{:S(2)}) async-start(), calls=%async_computation.10 | async-start | bytes 3686400 | tf_op jit(solution)/shard_map/all_gather | solution.py:230
  282.5 182.5 %all-gather.24.cloned.1.call-start = ((), (), s32[]{:S(2)}) async-start(), calls=%async_computation.11 | async-start | bytes 11943936 | tf_op jit(solution)/shard_map/all_gather | solution.py:155
  283.2 334.8 %all-gather.26.cloned.1.call-start = ((), (), s32[]{:S(2)}) async-start(), calls=%async_computation.12 | async-start | bytes 11943936 | tf_op jit(solution)/shard_map/all_gather | solution.py:156
  284.0 487.0 %all-gather.28.cloned.1.call-start = ((), (), s32[]{:S(2)}) async-start(), calls=%async_computation.13 | async-start | bytes 11943936 | tf_op jit(solution)/shard_map/all_gather | solution.py:157
  284.5 534.5 %reduce-scatter.7.cloned.1.call-start = ((), (), s32[]{:S(2)}) async-start(), calls=%async_computation.14 | async-start | bytes 3686400 | tf_op jit(solution)/shard_map/reduce_scatter | solution.py:236
  784.0 35.1 %copy-start.96 = (f32[2304]{0:T(1024)S(1)}, f32[2304]{0:T(1024)}, u32[]{:S(2)}) copy-start(f32[2304]{0:T(1024)} %get-tuple-element.18) | copy-start | bytes 27652
  784.0 67.1 %all-gather.30.cloned.1.call-start = ((), (), s32[]{:S(2)}) async-start(), calls=%async_computation.15 | async-start | bytes 3686400 | tf_op jit(solution)/shard_map/all_gather | solution.py:242
  823.5 119.5 %reduce-scatter.9.cloned.1.call-start = ((), (), s32[]{:S(2)}) async-start(), calls=%async_computation.16 | async-start | bytes 3686400 | tf_op jit(solution)/shard_map/reduce_scatter | solution.py:249
  871.4 15.2 copy-start.15
  906.1 36.9 %copy-start.79 = (f32[2304]{0:T(1024)S(1)}, f32[2304]{0:T(1024)}, u32[]{:S(2)}) copy-start(f32[2304]{0:T(1024)} %copy-done.78) | copy-start | bytes 27652
  906.1 36.9 %copy-start.98 = (f32[2304]{0:T(1024)S(1)}, f32[2304]{0:T(1024)}, u32[]{:S(2)}) copy-start(f32[2304]{0:T(1024)} %get-tuple-element.19) | copy-start | bytes 27652
  906.1 36.9 %copy-start.123 = (f32[160]{0:T(256)S(1)}, f32[160]{0:T(256)}, u32[]{:S(2)}) copy-start(f32[160]{0:T(256)} %copy-done.122) | copy-start | bytes 1924
  906.1 39.1 %copy-start.129 = (f32[160]{0:T(256)S(1)}, f32[160]{0:T(256)}, u32[]{:S(2)}) copy-start(f32[160]{0:T(256)} %copy-done.128) | copy-start | bytes 1924
  906.1 39.1 %copy-start.138 = (f32[160]{0:T(256)S(1)}, f32[160]{0:T(256)}, u32[]{:S(2)}) copy-start(f32[160]{0:T(256)} %get-tuple-element.74) | copy-start | bytes 1924
  906.1 73.3 %all-gather.32.cloned.1.call-start = ((), (), s32[]{:S(2)}) async-start(), calls=%async_computation.17 | async-start | bytes 3686400 | tf_op jit(solution)/shard_map/all_gather | solution.py:254
  951.8 208.6 %all-reduce.9.cloned.1.call-start = ((), (), s32[]{:S(2)}) async-start(), calls=%async_computation.20 | async-start | bytes 16515072 | tf_op jit(solution)/shard_map/psum | solution.py:315
  961.0 23.2 %copy-start.55 = (bf16[1,16,2304]{2,0,1:T(2,128)(2,1)S(1)}, bf16[1,16,2304]{2,0,1:T(2,128)(2,1)}, u32[]{:S(2)}) copy-start(bf16[1,16,2304]{2,0,1:T(2,128)(2,1)} %fusion.86) | copy-start | bytes 221188
  1007.3 265.0 %all-reduce.11.cloned.1.call-start = ((), (), s32[]{:S(2)}) async-start(), calls=%async_computation.21 | async-start | bytes 4325376 | tf_op jit(solution)/shard_map/psum | solution.py:309
  1021.5 288.8 %reduce-scatter.11.cloned.1.call-start = ((), (), s32[]{:S(2)}) async-start(), calls=%async_computation.18 | async-start | bytes 3686400 | tf_op jit(solution)/shard_map/reduce_scatter | solution.py:297
  1034.9 551.8 %all-reduce.7.cloned.1.call-start = ((), (), s32[]{:S(2)}) async-start(), calls=%async_computation.19 | async-start | bytes 16515072 | tf_op jit(solution)/shard_map/psum | solution.py:314
  1275.5 34.8 %copy-start.6 = (bf16[160,2304]{1,0:T(8,128)(2,1)S(1)}, bf16[160,2304]{1,0:T(8,128)(2,1)}, u32[]{:S(2)}) copy-start(bf16[160,2304]{1,0:T(8,128)(2,1)} %param.27) | copy-start | bytes 2211844
  1275.5 34.8 %copy-start.95 = (f32[2304]{0:T(1024)S(1)}, f32[2304]{0:T(1024)}, u32[]{:S(2)}) copy-start(f32[2304]{0:T(1024)} %copy-done.94) | copy-start | bytes 27652
  1280.9 30.8 %copy-start.18 = (f32[160,2304]{1,0:T(8,128)S(1)}, f32[160,2304]{1,0:T(8,128)}, u32[]{:S(2)}) copy-start(f32[160,2304]{1,0:T(8,128)} %copy-done.17) | copy-start | bytes 4423684
  1280.9 30.8 %copy-start.131 = (f32[160]{0:T(256)S(1)}, f32[160]{0:T(256)}, u32[]{:S(2)}) copy-start(f32[160]{0:T(256)} %copy-done.130) | copy-start | bytes 1924
  1280.9 30.8 %copy-start.137 = (f32[160]{0:T(256)S(1)}, f32[160]{0:T(256)}, u32[]{:S(2)}) copy-start(f32[160]{0:T(256)} %get-tuple-element.70) | copy-start | bytes 1924
  (109 other events, 446.1 us)
Sparse Core Ops, SparseCore 0:
  13.2 30.1 all-gather.11
  45.5 52.0 all-gather.17
  99.8 39.6 all-gather.15
  141.5 39.8 all-gather.13
  183.4 50.8 all-gather.19
  240.5 35.2 reduce-scatter.4
  282.6 27.4 all-gather.21
  312.4 152.4 all-gather.23
  467.3 150.6 all-gather.25
  620.3 150.6 all-gather.27
  784.1 34.9 reduce-scatter.6
  823.6 27.4 all-gather.29
  906.2 36.7 reduce-scatter.8
  951.9 27.4 all-gather.31
  1007.4 152.8 all-reduce.8
  1165.8 106.4 all-reduce.10
  1274.7 35.5 reduce-scatter.10
  1316.4 270.3 all-reduce.6
